TPU v7x, 32 devices: a whole 2x2x4 slice. The times are simulated.
32 devices in a mesh: band: 4 (over z), roster: 8 (over y, x, core).
Axes of the slice: x: 2, y: 2, z: 4, core: 2. Of those that a mesh axis runs over, the one named last changes fastest.
Arguments:
- tiles: bfloat16 [4, 8, 6, 256, 256], P('band', 'roster'), as said below
- tile_slots: int32 [4, 8, 6], P('band', 'roster'), may hold values from 0 to 5, each once within a row
- tile_count: int32 [4, 8], P('band', 'roster'), may hold values from 1 to 6, as said below
- costs: float32 [6144, 128], P('roster'), may hold values from 1000 to 10000
- primal_start: float32 [6144, 128], P('roster'), may hold values from 0 to 1
- dual_start: float32 [2048, 128], P('band'), may hold values from 0.5 to 4
Outputs:
- primal: float32 [6144, 128], P('roster')
- dual: float32 [2048, 128], P('band')
Inputs may be any that keep to these rules, and one draw needn't show every extreme that they name: `tile_slots`: each device's slots list every tile position once; slot s is in use where s < tile_count. `tile_count`: some device uses all 6 slots. `tiles`: entries are zero or positive.
All inputs are finite; a program needn't handle non-finite values.
Results may differ from a plain program's by a relative error of at most 0.0003.
Values sent between devices are 32-bit elements; how exact they have to be, the bound alone decides.
A program may use at most 64 MiB of HBM per device.

v0:
```python
import jax
import jax.numpy as jnp
from jax import lax
from jax.sharding import PartitionSpec as P

ROUNDS = 3
ITERS = 4
HIGH = lax.Precision.HIGHEST
eps = 1e-06


def shards(tiles, tile_slots, tile_count, costs, primal_start, dual_start):
    tile_block = tiles[0, 0]
    slots = tile_slots[0, 0]
    count = tile_count[0, 0]
    tile = tile_block.shape[1]
    rows = dual_start.shape[0]
    cols = costs.shape[0]
    row_tiles = rows // tile
    col_tiles = cols // tile
    row_index = slots // col_tiles
    col_index = slots % col_tiles
    active = (jnp.arange(slots.shape[0], dtype=jnp.int32) < count).astype(jnp.float32)
    row_hot = (row_index[None, :] == jnp.arange(row_tiles, dtype=jnp.int32)[:, None]).astype(
        jnp.float32
    )
    col_hot = (col_index[None, :] == jnp.arange(col_tiles, dtype=jnp.int32)[:, None]).astype(
        jnp.float32
    )

    def scale_tiles(row_scale, col_scale):
        row_part = row_scale.reshape(row_tiles, tile)[row_index]
        col_part = col_scale.reshape(col_tiles, tile)[col_index]
        return (
            tile_block.astype(jnp.float32)
            * row_part[:, :, None]
            * col_part[:, None, :]
            * active[:, None, None]
        )

    row_scale = jnp.ones((rows,), jnp.float32)
    col_scale = jnp.ones((cols,), jnp.float32)
    for turn in range(ROUNDS):
        magnitude = jnp.abs(scale_tiles(row_scale, col_scale))
        slot_rows = jnp.max(magnitude, axis=2)
        slot_cols = jnp.max(magnitude, axis=1)
        row_peak = jnp.max(row_hot[:, :, None] * slot_rows[None], axis=1).reshape(-1)
        col_peak = jnp.max(col_hot[:, :, None] * slot_cols[None], axis=1).reshape(-1)
        row_peak = lax.pmax(row_peak, "roster")
        col_peak = lax.pmax(col_peak, "band")
        row_scale = row_scale / jnp.sqrt(row_peak + eps)
        col_scale = col_scale / jnp.sqrt(col_peak + eps)
    scaled = scale_tiles(row_scale, col_scale)
    squares = lax.psum(jnp.sum(scaled * scaled), ("band", "roster"))
    eta = 0.9 / jnp.sqrt(squares + eps)
    scen = costs.shape[1]
    col_full = col_scale[:, None]
    row_full = row_scale[:, None]
    cost_t = costs * col_full
    upper = 1.0 / col_full
    primal = primal_start / col_full
    dual = dual_start / row_full
    for step in range(ITERS):
        dual_slots = dual.reshape(row_tiles, tile, scen)[row_index]
        back_terms = jnp.einsum("sij,sik->sjk", scaled, dual_slots, precision=HIGH)
        g_local = jnp.einsum("cs,sjk->cjk", col_hot, back_terms, precision=HIGH).reshape(cols, scen)
        g_whole = lax.psum(g_local, "band")
        primal_next = jnp.clip(primal - eta * (cost_t - g_whole), 0.0, upper)
        extrapolated = 2.0 * primal_next - primal
        primal_slots = extrapolated.reshape(col_tiles, tile, scen)[col_index]
        fore_terms = jnp.einsum("sij,sjk->sik", scaled, primal_slots, precision=HIGH)
        h_local = jnp.einsum("rs,sik->rik", row_hot, fore_terms, precision=HIGH).reshape(rows, scen)
        share = rows // lax.axis_size("roster")
        begin = lax.axis_index("roster") * share
        h_share = lax.psum_scatter(h_local, "roster", scatter_dimension=0, tiled=True)
        own_dual = lax.dynamic_slice_in_dim(dual, begin, share, 0)
        own_rows = lax.dynamic_slice_in_dim(row_full, begin, share, 0)
        dual_share = own_dual + eta * (own_rows - h_share)
        dual = lax.all_gather(dual_share, "roster", axis=0, tiled=True)
        primal = primal_next
    return (primal, dual)


def solution(mesh):
    placed = (
        P("band", "roster", None, None, None),
        P("band", "roster", None),
        P("band", "roster"),
        P("roster", None),
        P("roster", None),
        P("band", None),
    )
    return jax.shard_map(
        shards,
        mesh=mesh,
        in_specs=placed,
        out_specs=(P("roster", None), P("band", None)),
        check_vma=False,
    )
```

profile of v0, /device:TPU:0, one launch (start us, length us, event | category | flops | bytes accessed | tf_op | source)
XLA Modules:
  0.0 466.0 jit_solution(17935510203944272796)
XLA Ops:
  10.5 1.8 fusion.3
  12.4 15.1 %pmax.43 = f32[512]{0:T(512)S(1)} all-reduce(f32[512]{0:T(512)S(1)} %bitcast.135), channel_id=1, replica_groups=mesh['band'=4,'roster'=8] {'roster'}, use_global_device_ids=true, to_apply=%region_5.6 | all-reduce | flops 512 | bytes 4096 | tf_op jit(solution)/shard_map/pmax | solution.py:49
  27.7 12.0 %pmax.42 = f32[768]{0:T(1024)S(1)} all-reduce(f32[768]{0:T(1024)S(1)} %reshape.279), channel_id=1, replica_groups=mesh['band'=4,'roster'=8] {'band'}, use_global_device_ids=true, to_apply=%region_2.3 | all-reduce | flops 768 | bytes 6144 | tf_op jit(solution)/shard_map/pmax | solution.py:50
  41.6 8.4 %pmax.44 = f32[768]{0:T(1024)S(1)} all-reduce(f32[768]{0:T(1024)S(1)} %reshape.283), channel_id=1, replica_groups=mesh['band'=4,'roster'=8] {'band'}, use_global_device_ids=true, to_apply=%region_8.9 | all-reduce | flops 768 | bytes 6144 | tf_op jit(solution)/shard_map/pmax | solution.py:50
  50.0 11.8 %pmax.45 = f32[512]{0:T(512)S(1)} all-reduce(f32[512]{0:T(512)S(1)} %bitcast.136), channel_id=1, replica_groups=mesh['band'=4,'roster'=8] {'roster'}, use_global_device_ids=true, to_apply=%region_11.12 | all-reduce | flops 512 | bytes 4096 | tf_op jit(solution)/shard_map/pmax | solution.py:49
  63.8 10.4 %pmax.46 = f32[768]{0:T(1024)S(1)} all-reduce(f32[768]{0:T(1024)S(1)} %reshape.287), channel_id=1, replica_groups=mesh['band'=4,'roster'=8] {'band'}, use_global_device_ids=true, to_apply=%region_14.15 | all-reduce | flops 768 | bytes 6144 | tf_op jit(solution)/shard_map/pmax | solution.py:50
  74.2 11.8 %pmax.47 = f32[512]{0:T(512)S(1)} all-reduce(f32[512]{0:T(512)S(1)} %bitcast.137), channel_id=1, replica_groups=mesh['band'=4,'roster'=8] {'roster'}, use_global_device_ids=true, to_apply=%region_17.18 | all-reduce | flops 512 | bytes 4096 | tf_op jit(solution)/shard_map/pmax | solution.py:49
  87.9 2.9 fusion.31
  92.8 1.2 fusion.34
  93.9 37.9 %psum.35 = f32[]{:T(128)} all-reduce(f32[]{:T(128)} %fusion.34), channel_id=1, replica_groups=mesh['band'=4,'roster'=8] {'band','roster'}, use_global_device_ids=true, to_apply=%region_19.20 | all-reduce | flops 1 | bytes 8 | tf_op jit(solution)/shard_map/psum | solution.py:54
  132.6 1.3 multiply_subtract_fusion.3
  134.5 1.8 fusion.29
  138.2 33.9 %reduce-scatter.5.cloned.1.call-done = f32[64,128]{1,0:T(8,128)} async-done(((f32[512,128]{1,0:T(8,128)}), f32[64,128]{1,0:T(8,128)}) %reduce-scatter.5.cloned.1.call-update) | async-done | bytes 32784 | tf_op jit(solution)/shard_map/reduce_scatter | solution.py:75
  172.8 9.7 %all_gather.12 = f32[512,128]{1,0:T(8,128)S(1)} all-gather(f32[64,128]{1,0:T(8,128)S(1)} %multiply_add_fusion.3), channel_id=1, replica_groups=mesh['band'=4,'roster'=8] {'roster'}, dimensions={0}, use_global_device_ids=true | all-gather | bytes 294912 | tf_op jit(solution)/shard_map/all_gather | solution.py:79
  183.2 3.0 fusion.27
  188.0 37.0 %all-reduce.7.cloned.1.call-done = f32[768,128]{1,0:T(8,128)} async-done(((f32[768,128]{1,0:T(8,128)}), f32[768,128]{1,0:T(8,128)}) %all-reduce.7.cloned.1.call-update) | async-done | bytes 393232 | tf_op jit(solution)/shard_map/psum | solution.py:67
  225.0 1.3 multiply_subtract_fusion.2
  226.9 1.8 fusion.25
  230.4 33.5 %reduce-scatter.7.cloned.1.call-done = f32[64,128]{1,0:T(8,128)} async-done(((f32[512,128]{1,0:T(8,128)}), f32[64,128]{1,0:T(8,128)}) %reduce-scatter.7.cloned.1.call-update) | async-done | bytes 32784 | tf_op jit(solution)/shard_map/reduce_scatter | solution.py:75
  264.8 9.4 %all_gather.13 = f32[512,128]{1,0:T(8,128)S(1)} all-gather(f32[64,128]{1,0:T(8,128)S(1)} %multiply_add_fusion.2), channel_id=1, replica_groups=mesh['band'=4,'roster'=8] {'roster'}, dimensions={0}, use_global_device_ids=true | all-gather | bytes 294912 | tf_op jit(solution)/shard_map/all_gather | solution.py:79
  274.8 3.0 fusion.23
  279.6 37.1 %all-reduce.9.cloned.1.call-done = f32[768,128]{1,0:T(8,128)} async-done(((f32[768,128]{1,0:T(8,128)}), f32[768,128]{1,0:T(8,128)}) %all-reduce.9.cloned.1.call-update) | async-done | bytes 393232 | tf_op jit(solution)/shard_map/psum | solution.py:67
  316.7 1.3 multiply_subtract_fusion.1
  318.6 1.8 fusion.21
  322.1 33.5 %reduce-scatter.9.cloned.1.call-done = f32[64,128]{1,0:T(8,128)} async-done(((f32[512,128]{1,0:T(8,128)}), f32[64,128]{1,0:T(8,128)}) %reduce-scatter.9.cloned.1.call-update) | async-done | bytes 32784 | tf_op jit(solution)/shard_map/reduce_scatter | solution.py:75
  356.5 9.5 %all_gather.14 = f32[512,128]{1,0:T(8,128)S(1)} all-gather(f32[64,128]{1,0:T(8,128)S(1)} %multiply_add_fusion.1), channel_id=1, replica_groups=mesh['band'=4,'roster'=8] {'roster'}, dimensions={0}, use_global_device_ids=true | all-gather | bytes 294912 | tf_op jit(solution)/shard_map/all_gather | solution.py:79
  366.6 3.0 fusion.19
  371.4 37.1 %all-reduce.11.cloned.1.call-done = f32[768,128]{1,0:T(8,128)} async-done(((f32[768,128]{1,0:T(8,128)}), f32[768,128]{1,0:T(8,128)}) %all-reduce.11.cloned.1.call-update) | async-done | bytes 393232 | tf_op jit(solution)/shard_map/psum | solution.py:67
  408.4 2.0 multiply_subtract_fusion
  411.1 1.8 fusion.17
  414.6 33.6 %reduce-scatter.11.cloned.1.call-done = f32[64,128]{1,0:T(8,128)} async-done(((f32[512,128]{1,0:T(8,128)}), f32[64,128]{1,0:T(8,128)}) %reduce-scatter.11.cloned.1.call-update) | async-done | bytes 32784 | tf_op jit(solution)/shard_map/reduce_scatter | solution.py:75
  449.0 9.2 %all_gather.15 = f32[512,128]{1,0:T(8,128)S(1)} all-gather(f32[64,128]{1,0:T(8,128)S(1)} %multiply_add_fusion), channel_id=1, replica_groups=mesh['band'=4,'roster'=8] {'roster'}, dimensions={0}, use_global_device_ids=true | all-gather | bytes 294912 | tf_op jit(solution)/shard_map/all_gather | solution.py:79
  (99 shorter events, 31.4 us)
Async XLA Ops:
  7.2 33.6 %copy-start = (bf16[1,1,6,256,256]{4,3,2,1,0:T(8,128)(2,1)S(1)}, bf16[1,1,6,256,256]{4,3,2,1,0:T(8,128)(2,1)}, u32[]{:S(2)}) copy-start(bf16[1,1,6,256,256]{4,3,2,1,0:T(8,128)(2,1)} %param.6) | copy-start | bytes 2359300
  7.2 125.4 %all-reduce.5.cloned.1.call-start = ((), (), s32[]{:S(2)}) async-start(), calls=%async_computation.4 | async-start | bytes 786432 | tf_op jit(solution)/shard_map/psum | solution.py:67
  41.4 45.7 %copy-start.3 = (f32[512,128]{1,0:T(8,128)S(1)}, f32[512,128]{1,0:T(8,128)}, u32[]{:S(2)}) copy-start(f32[512,128]{1,0:T(8,128)} %param.11) | copy-start | bytes 786436
  92.7 39.9 %copy-start.1 = (f32[768,128]{1,0:T(8,128)S(1)}, f32[768,128]{1,0:T(8,128)}, u32[]{:S(2)}) copy-start(f32[768,128]{1,0:T(8,128)} %param.9) | copy-start | bytes 1179652
  92.7 39.9 %copy-start.2 = (f32[768,128]{1,0:T(8,128)S(1)}, f32[768,128]{1,0:T(8,128)}, u32[]{:S(2)}) copy-start(f32[768,128]{1,0:T(8,128)} %param.10) | copy-start | bytes 1179652
  92.7 79.3 %reduce-scatter.5.cloned.1.call-start = ((), (), s32[]{:S(2)}) async-start(), calls=%async_computation.5 | async-start | bytes 294912 | tf_op jit(solution)/shard_map/reduce_scatter | solution.py:75
  138.0 87.0 %all-reduce.7.cloned.1.call-start = ((), (), s32[]{:S(2)}) async-start(), calls=%async_computation.6 | async-start | bytes 786432 | tf_op jit(solution)/shard_map/psum | solution.py:67
  187.9 76.1 %reduce-scatter.7.cloned.1.call-start = ((), (), s32[]{:S(2)}) async-start(), calls=%async_computation.7 | async-start | bytes 294912 | tf_op jit(solution)/shard_map/reduce_scatter | solution.py:75
  230.4 86.3 %all-reduce.9.cloned.1.call-start = ((), (), s32[]{:S(2)}) async-start(), calls=%async_computation.8 | async-start | bytes 786432 | tf_op jit(solution)/shard_map/psum | solution.py:67
  279.6 76.1 %reduce-scatter.9.cloned.1.call-start = ((), (), s32[]{:S(2)}) async-start(), calls=%async_computation.9 | async-start | bytes 294912 | tf_op jit(solution)/shard_map/reduce_scatter | solution.py:75
  322.1 86.4 %all-reduce.11.cloned.1.call-start = ((), (), s32[]{:S(2)}) async-start(), calls=%async_computation.10 | async-start | bytes 786432 | tf_op jit(solution)/shard_map/psum | solution.py:67
  371.3 76.8 %reduce-scatter.11.cloned.1.call-start = ((), (), s32[]{:S(2)}) async-start(), calls=%async_computation.11 | async-start | bytes 294912 | tf_op jit(solution)/shard_map/reduce_scatter | solution.py:75
Sparse Core Ops, SparseCore 0:
  92.8 33.2 all-reduce.4
  138.1 33.8 reduce-scatter.4
  188.0 36.9 all-reduce.6
  230.5 33.4 reduce-scatter.6
  279.7 36.9 all-reduce.8
  322.2 33.4 reduce-scatter.8
  371.5 36.9 all-reduce.10
  414.7 33.4 reduce-scatter.10
where the time goes:
time: 475 us; the launch traced here: 466 us
  waiting for transfers between devices  246 us (52%)
  blocking collectives  145 us (31%)
  matrix products  26.8 us (6%)
  local copies, waits for them, and re-layouts  16.3 us (3%)
  between operations  16.1 us (3%)
  other arithmetic  15.4 us (3%)
    reduce_scatter x4, waiting for transfers between devices, shards(): lax.psum_scatter(h_local, 'roster', scatter_dimension=0, tiled=True)  135 us
    psum x4, waiting for transfers between devices, shards(): g_whole = lax.psum(g_local, 'band')  111 us
    pmax x3, blocking collectives, shards(): row_peak = lax.pmax(row_peak, 'roster')  38.7 us
    psum x1, blocking collectives, shards(): squares = lax.psum(jnp.sum(scaled * scaled), ('band', 'roster'))  37.9 us
    all_gather x4, blocking collectives, shards(): dual = lax.all_gather(dual_share, 'roster', axis=0, tiled=True)  37.8 us
    pmax x3, blocking collectives, shards(): col_peak = lax.pmax(col_peak, 'band')  30.7 us
    dot_general x4, matrix products, shards(): back_terms = jnp.einsum('sij,sik->sjk', scaled, dual_slots, precision=HIGH)  11.8 us
  transfers between devices with their start and end apart: 8, of which 7 were waited for; matrix products, arithmetic and copies ran while one was open for 0% of the time, Pallas kernels for 0%

commit v1 on v0

--- a/solution.py
+++ b/solution.py
@@ -7,6 +7,12 @@
 ITERS = 4
 HIGH = lax.Precision.HIGHEST
 eps = 1e-06
+
+
+def match_scenes(state, d0):
+    state = jnp.moveaxis(state, 0, d0)
+    oldest = state.shape
+    return state.reshape(*oldest[:d0], oldest[d0] * oldest[d0 + 1], *oldest[d0 + 2 :])
 
 
 def shards(tiles, tile_slots, tile_count, costs, primal_start, dual_start):
@@ -76,7 +82,33 @@
         own_dual = lax.dynamic_slice_in_dim(dual, begin, share, 0)
         own_rows = lax.dynamic_slice_in_dim(row_full, begin, share, 0)
         dual_share = own_dual + eta * (own_rows - h_share)
-        dual = lax.all_gather(dual_share, "roster", axis=0, tiled=True)
+        fan = lax.axis_size("roster")
+        fields = tuple(((tick, (tick + 1) % fan) for tick in range(fan)))
+        all_values, everything = ([], [])
+        buffers = tuple(((i, to_i) for to_i, i in fields))
+        dev = 0
+        while dev < fan - 1:
+            if dev % 2 == 0:
+                all_values.append(
+                    lax.ppermute(
+                        all_values[-1] if all_values else dual_share,
+                        axis_name="roster",
+                        perm=fields,
+                    )
+                )
+            else:
+                everything.append(
+                    lax.ppermute(
+                        everything[-1] if everything else dual_share,
+                        axis_name="roster",
+                        perm=buffers,
+                    )
+                )
+            dev += 1
+        next_value = jnp.stack([*all_values[::-1], dual_share, *everything])
+        back = lax.axis_index("roster") - len(all_values)
+        next_value = next_value[(jnp.arange(fan) - back) % fan]
+        dual = match_scenes(next_value, 0)
         primal = primal_next
     return (primal, dual)
 

time: 475 us -> 514 us (1.082)
  waiting for transfers between devices: 246 us -> 287 us
  blocking collectives: 145 us -> 107 us
  starting transfers between devices: 0.33 us -> 33 us
    all_gather x4 -> x0, blocking collectives: 37.8 us -> none  [shards(): dual = lax.all_gather(dual_share, 'roster', axis=0, tiled=True)]
    ppermute x0 -> x28, waiting for transfers between devices: none -> 37.1 us  [the longest x16 36.8 us: shards(): lax.ppermute(all_values[-1] if all_values else dual_share, axis_name='ros...]
    ppermute x0 -> x28, starting transfers between devices: none -> 32.6 us  [the longest x12 32.1 us: shards(): lax.ppermute(everything[-1] if everything else dual_share, axis_name='ros...]
  transfers between devices with their start and end apart: 8 -> 36, of which waited for: 7 -> 26; matrix products, arithmetic and copies ran while one was open for 0% -> 0% of each run, Pallas kernels for 0% -> 0%
where the time goes in v1:
time: 514 us; the launch traced here: 504 us
  waiting for transfers between devices  287 us (56%)
  blocking collectives  107 us (21%)
  starting transfers between devices  33 us (6%)
  matrix products  26.8 us (5%)
  local copies, waits for them, and re-layouts  18.7 us (4%)
  between operations  16.4 us (3%)
  other arithmetic  15.5 us (3%)
    reduce_scatter x4, waiting for transfers between devices, shards(): lax.psum_scatter(h_local, 'roster', scatter_dimension=0, tiled=True)  134 us
    psum x4, waiting for transfers between devices, shards(): g_whole = lax.psum(g_local, 'band')  115 us
    pmax x3, blocking collectives, shards(): row_peak = lax.pmax(row_peak, 'roster')  38.7 us
    psum x1, blocking collectives, shards(): squares = lax.psum(jnp.sum(scaled * scaled), ('band', 'roster'))  38 us
    ppermute x16, waiting for transfers between devices, shards(): lax.ppermute(all_values[-1] if all_values else dual_share, axis_name='ros...  36.8 us
    ppermute x12, starting transfers between devices, shards(): lax.ppermute(everything[-1] if everything else dual_share, axis_name='ros...  32.1 us
    pmax x3, blocking collectives, shards(): col_peak = lax.pmax(col_peak, 'band')  30.7 us
    dot_general x4, matrix products, shards(): back_terms = jnp.einsum('sij,sik->sjk', scaled, dual_slots, precision=HIGH)  11.8 us
  transfers between devices with their start and end apart: 36, of which 26 were waited for; matrix products, arithmetic and copies ran while one was open for 0% of the time, Pallas kernels for 0%

profile of v1, /device:TPU:0, one launch (start us, length us, event | category | flops | bytes accessed | tf_op | source)
XLA Modules:
  0.0 504.3 jit_solution(9852510937252173067)
XLA Ops:
  12.4 15.1 %pmax.43 = f32[512]{0:T(512)S(1)} all-reduce(f32[512]{0:T(512)S(1)} %bitcast.209), channel_id=1, replica_groups=mesh['band'=4,'roster'=8] {'roster'}, use_global_device_ids=true, to_apply=%region_5.6 | all-reduce | flops 512 | bytes 4096 | tf_op jit(solution)/shard_map/pmax | solution.py:55
  27.7 12.0 %pmax.42 = f32[768]{0:T(1024)S(1)} all-reduce(f32[768]{0:T(1024)S(1)} %reshape.331), channel_id=1, replica_groups=mesh['band'=4,'roster'=8] {'band'}, use_global_device_ids=true, to_apply=%region_2.3 | all-reduce | flops 768 | bytes 6144 | tf_op jit(solution)/shard_map/pmax | solution.py:56
  41.6 8.4 %pmax.44 = f32[768]{0:T(1024)S(1)} all-reduce(f32[768]{0:T(1024)S(1)} %reshape.335), channel_id=1, replica_groups=mesh['band'=4,'roster'=8] {'band'}, use_global_device_ids=true, to_apply=%region_8.9 | all-reduce | flops 768 | bytes 6144 | tf_op jit(solution)/shard_map/pmax | solution.py:56
  50.0 11.8 %pmax.45 = f32[512]{0:T(512)S(1)} all-reduce(f32[512]{0:T(512)S(1)} %bitcast.210), channel_id=1, replica_groups=mesh['band'=4,'roster'=8] {'roster'}, use_global_device_ids=true, to_apply=%region_11.12 | all-reduce | flops 512 | bytes 4096 | tf_op jit(solution)/shard_map/pmax | solution.py:55
  63.8 10.4 %pmax.46 = f32[768]{0:T(1024)S(1)} all-reduce(f32[768]{0:T(1024)S(1)} %reshape.339), channel_id=1, replica_groups=mesh['band'=4,'roster'=8] {'band'}, use_global_device_ids=true, to_apply=%region_14.15 | all-reduce | flops 768 | bytes 6144 | tf_op jit(solution)/shard_map/pmax | solution.py:56
  74.2 11.8 %pmax.47 = f32[512]{0:T(512)S(1)} all-reduce(f32[512]{0:T(512)S(1)} %bitcast.211), channel_id=1, replica_groups=mesh['band'=4,'roster'=8] {'roster'}, use_global_device_ids=true, to_apply=%region_17.18 | all-reduce | flops 512 | bytes 4096 | tf_op jit(solution)/shard_map/pmax | solution.py:55
  87.9 2.9 fusion.31
  93.9 38.0 %psum.35 = f32[]{:T(128)} all-reduce(f32[]{:T(128)} %fusion.34), channel_id=1, replica_groups=mesh['band'=4,'roster'=8] {'band','roster'}, use_global_device_ids=true, to_apply=%region_19.20 | all-reduce | flops 1 | bytes 8 | tf_op jit(solution)/shard_map/psum | solution.py:60
  138.2 33.8 %reduce-scatter.5.cloned.1.call-done = f32[64,128]{1,0:T(8,128)} async-done(((f32[512,128]{1,0:T(8,128)}), f32[64,128]{1,0:T(8,128)}) %reduce-scatter.5.cloned.1.call-update) | async-done | bytes 32784 | tf_op jit(solution)/shard_map/reduce_scatter | solution.py:81
  173.3 4.2 collective-permute-done
  177.5 2.6 collective-permute-start.4
  182.1 2.7 collective-permute-start.5
  191.8 2.9 fusion.27
  196.7 38.3 %all-reduce.7.cloned.1.call-done = f32[768,128]{1,0:T(8,128)} async-done(((f32[768,128]{1,0:T(8,128)}), f32[768,128]{1,0:T(8,128)}) %all-reduce.7.cloned.1.call-update) | async-done | bytes 393232 | tf_op jit(solution)/shard_map/psum | solution.py:73
  240.4 33.5 %reduce-scatter.7.cloned.1.call-done = f32[64,128]{1,0:T(8,128)} async-done(((f32[512,128]{1,0:T(8,128)}), f32[64,128]{1,0:T(8,128)}) %reduce-scatter.7.cloned.1.call-update) | async-done | bytes 32784 | tf_op jit(solution)/shard_map/reduce_scatter | solution.py:81
  274.8 4.2 collective-permute-done.7
  279.0 2.6 collective-permute-start.11
  283.6 2.6 collective-permute-start.12
  287.8 2.8 collective-permute-start.13
  293.4 3.0 fusion.23
  298.2 38.3 %all-reduce.9.cloned.1.call-done = f32[768,128]{1,0:T(8,128)} async-done(((f32[768,128]{1,0:T(8,128)}), f32[768,128]{1,0:T(8,128)}) %all-reduce.9.cloned.1.call-update) | async-done | bytes 393232 | tf_op jit(solution)/shard_map/psum | solution.py:73
  341.9 33.5 %reduce-scatter.9.cloned.1.call-done = f32[64,128]{1,0:T(8,128)} async-done(((f32[512,128]{1,0:T(8,128)}), f32[64,128]{1,0:T(8,128)}) %reduce-scatter.9.cloned.1.call-update) | async-done | bytes 32784 | tf_op jit(solution)/shard_map/reduce_scatter | solution.py:81
  376.3 4.2 collective-permute-done.14
  380.5 2.6 collective-permute-start.18
  385.1 2.6 collective-permute-start.19
  389.3 2.8 collective-permute-start.20
  394.9 3.0 fusion.19
  399.7 38.3 %all-reduce.11.cloned.1.call-done = f32[768,128]{1,0:T(8,128)} async-done(((f32[768,128]{1,0:T(8,128)}), f32[768,128]{1,0:T(8,128)}) %all-reduce.11.cloned.1.call-update) | async-done | bytes 393232 | tf_op jit(solution)/shard_map/psum | solution.py:73
  444.2 33.6 %reduce-scatter.11.cloned.1.call-done = f32[64,128]{1,0:T(8,128)} async-done(((f32[512,128]{1,0:T(8,128)}), f32[64,128]{1,0:T(8,128)}) %reduce-scatter.11.cloned.1.call-update) | async-done | bytes 32784 | tf_op jit(solution)/shard_map/reduce_scatter | solution.py:81
  478.6 4.2 collective-permute-done.21
  482.8 2.6 collective-permute-start.25
  487.4 2.6 collective-permute-start.26
  (188 shorter events, 75.6 us)
Async XLA Ops:
  7.2 125.4 %all-reduce.5.cloned.1.call-start = ((), (), s32[]{:S(2)}) async-start(), calls=%async_computation.4 | async-start | bytes 786432 | tf_op jit(solution)/shard_map/psum | solution.py:73
  92.7 79.3 %reduce-scatter.5.cloned.1.call-start = ((), (), s32[]{:S(2)}) async-start(), calls=%async_computation.5 | async-start | bytes 294912 | tf_op jit(solution)/shard_map/reduce_scatter | solution.py:81
  138.0 96.9 %all-reduce.7.cloned.1.call-start = ((), (), s32[]{:S(2)}) async-start(), calls=%async_computation.6 | async-start | bytes 786432 | tf_op jit(solution)/shard_map/psum | solution.py:73
  172.8 4.7 collective-permute-start
  177.5 4.5 collective-permute-start.1
  177.5 4.6 collective-permute-start.4
  182.1 4.2 collective-permute-start.2
  182.1 4.3 collective-permute-start.5
  186.3 4.2 collective-permute-start.3
  186.4 4.2 collective-permute-start.6
  196.6 77.3 %reduce-scatter.7.cloned.1.call-start = ((), (), s32[]{:S(2)}) async-start(), calls=%async_computation.7 | async-start | bytes 294912 | tf_op jit(solution)/shard_map/reduce_scatter | solution.py:81
  240.3 96.1 %all-reduce.9.cloned.1.call-start = ((), (), s32[]{:S(2)}) async-start(), calls=%async_computation.8 | async-start | bytes 786432 | tf_op jit(solution)/shard_map/psum | solution.py:73
  274.7 4.2 collective-permute-start.7
  279.0 4.6 collective-permute-start.8
  279.0 4.6 collective-permute-start.11
  283.6 4.2 collective-permute-start.12
  287.8 4.4 collective-permute-start.13
  298.1 77.3 %reduce-scatter.9.cloned.1.call-start = ((), (), s32[]{:S(2)}) async-start(), calls=%async_computation.9 | async-start | bytes 294912 | tf_op jit(solution)/shard_map/reduce_scatter | solution.py:81
  341.9 96.2 %all-reduce.11.cloned.1.call-start = ((), (), s32[]{:S(2)}) async-start(), calls=%async_computation.10 | async-start | bytes 786432 | tf_op jit(solution)/shard_map/psum | solution.py:73
  376.3 4.2 collective-permute-start.14
  380.5 4.5 collective-permute-start.15
  380.5 4.6 collective-permute-start.18
  385.1 4.2 collective-permute-start.19
  389.3 4.2 collective-permute-start.17
  389.3 4.4 collective-permute-start.20
  399.7 78.1 %reduce-scatter.11.cloned.1.call-start = ((), (), s32[]{:S(2)}) async-start(), calls=%async_computation.11 | async-start | bytes 294912 | tf_op jit(solution)/shard_map/reduce_scatter | solution.py:81
  478.6 4.2 collective-permute-start.21
  482.8 4.5 collective-permute-start.22
  482.8 4.5 collective-permute-start.25
  487.4 4.2 collective-permute-start.23
  487.4 4.2 collective-permute-start.26
  491.6 4.3 collective-permute-start.27
  (8 other events, 176.2 us)
Sparse Core Ops, SparseCore 0:
  92.8 33.2 all-reduce.4
  138.2 33.7 reduce-scatter.4
  196.7 38.1 all-reduce.6
  240.4 33.4 reduce-scatter.6
  298.2 38.1 all-reduce.8
  342.0 33.4 reduce-scatter.8
  399.8 38.1 all-reduce.10
  444.3 33.4 reduce-scatter.10
